TPU v7x, 32 devices: a whole 2x2x4 slice. The times are simulated.
32 devices in a mesh: groups: 2 (over y), ctx: 4 (over z), exp: 2 (over x), head: 2 (over core).
Axes of the slice: x: 2, y: 2, z: 4, core: 2. Of those that a mesh axis runs over, the one named last changes fastest.
Arguments:
- latent: bfloat16 [256, 576], P(('groups', 'ctx')), parts along dimension 0, may hold values from -5 to 5
- query: bfloat16 [256, 3072], P(('groups', 'ctx'), ('exp', 'head')), parts along dimension 0, may hold values from -30 to 30
- w_uk: bfloat16 [512, 2048], P(None, ('exp', 'head')), may hold values from -0.25 to 0.25
- w_uv: bfloat16 [512, 2048], P(None, ('exp', 'head')), may hold values from -0.25 to 0.25
- w_o: bfloat16 [2048, 3584], P(('exp', 'head'), 'ctx'), may hold values from -0.5 to 0.5
- resid: bfloat16 [256, 3584], P(('groups', 'ctx', 'exp', 'head')), parts along dimension 0, may hold values from -6 to 6
- norm_gain: float32 [3584], replicated, may hold values from 0.1 to 1.9
- w_gate: bfloat16 [4, 3584, 2048], P(('exp', 'head'), None, 'ctx'), may hold values from -0.09375 to 0.09375
- w_up: bfloat16 [4, 3584, 2048], P(('exp', 'head'), None, 'ctx'), may hold values from -0.09375 to 0.09375
- w_down: bfloat16 [4, 2048, 3584], P(('exp', 'head'), None, 'ctx'), may hold values from -0.125 to 0.125
- expert_ids: int32 [256, 2], P(('groups', 'ctx', 'exp', 'head')), parts along dimension 0, may hold values from 0 to 3, all different within a row; in each aligned block of 8 rows (0 to 7, 8 to 15, ...) at most 8 rows name the same one
- route_weights: float32 [256, 2], P(('groups', 'ctx', 'exp', 'head')), parts along dimension 0, may hold values from 0.2 to 1
Outputs:
- layer_out: bfloat16 [256, 3584], P(('groups', 'ctx', 'exp', 'head')), parts along dimension 0
There are 2 independent parts, one for each index of `groups`. A program takes and returns all parts, laid end to end along the dimension named above; an argument that names none is the same for every part. Nothing has to cross between parts.
Inputs may be any that keep to these rules, and one draw needn't show every extreme that they name: `expert_ids`: each token names 2 different experts; within each aligned block of 8 tokens no expert is named more than 8 times, a bound that some block reaches.
All inputs are finite; a program needn't handle non-finite values.
Results may differ from a plain program's by a relative error of at most 0.014.
Values may be sent and summed in bfloat16 or wider, within the bound.
A program may use at most 64 MiB of HBM per device.

v0:
```python
import math
import jax
import jax.numpy as jnp
from jax import lax
from jax.sharding import PartitionSpec as P

D = 3584
NOPE = 128
ROPE = 64
LATENT = 512


def shards(
    latent,
    query,
    w_uk,
    w_uv,
    w_o,
    resid,
    norm_gain,
    w_gate,
    w_up,
    w_down,
    expert_ids,
    route_weights,
):
    qblock = query.shape[0]
    head_width = NOPE + ROPE
    heads_here = query.shape[1] // head_width
    nope_span = heads_here * NOPE
    score_scale = 1.0 / math.sqrt(head_width)
    query_all = query.reshape(qblock, heads_here, head_width)
    query_nope = query_all[:, :, :NOPE]
    query_rope = query_all[:, :, NOPE:]
    query_pos = lax.axis_index("ctx") * qblock + jnp.arange(qblock, dtype=jnp.int32)
    shard_rows = lax.all_gather(latent, "ctx", axis=0, tiled=True)
    piece_rows = shard_rows.shape[0]
    compressed = shard_rows[:, :LATENT]
    key_nope = (
        jnp.dot(compressed, w_uk, preferred_element_type=jnp.float32)
        .astype(jnp.bfloat16)
        .reshape(piece_rows, heads_here, NOPE)
    )
    values = (
        jnp.dot(compressed, w_uv, preferred_element_type=jnp.float32)
        .astype(jnp.bfloat16)
        .reshape(piece_rows, heads_here, NOPE)
    )
    run_max = jnp.full((qblock, heads_here), -1e30, jnp.float32)
    piece_rows = key_nope.shape[0]
    scores = jnp.einsum("qhd,khd->qhk", query_nope, key_nope, preferred_element_type=jnp.float32)
    scores = (
        scores
        + jnp.einsum(
            "qhd,kd->qhk", query_rope, shard_rows[:, LATENT:], preferred_element_type=jnp.float32
        )
    ) * score_scale
    key_pos = jnp.arange(piece_rows, dtype=jnp.int32)
    allowed = (key_pos[None, :] <= query_pos[:, None])[:, None, :]
    new_max = jnp.maximum(run_max, jnp.max(jnp.where(allowed, scores, -1e30), axis=2))
    exponent = jnp.where(allowed, jnp.exp(scores - new_max[:, :, None]), 0.0)
    run_sum = jnp.sum(exponent, axis=2)
    weighted_sum = jnp.einsum(
        "qhk,khd->qhd", exponent.astype(jnp.bfloat16), values, preferred_element_type=jnp.float32
    )
    attn_state = (new_max, run_sum, weighted_sum)
    run_max, run_sum, weighted_sum = attn_state
    attended = (weighted_sum / run_sum[:, :, None]).astype(jnp.bfloat16).reshape(qblock, nope_span)
    tok_dev = resid.shape[0]
    ctx_count = lax.axis_size("ctx")
    partial_value = jnp.dot(
        lax.all_gather(attended, "ctx", axis=0, tiled=True), w_o, preferred_element_type=jnp.float32
    )
    partial_value = partial_value.astype(jnp.bfloat16).reshape(ctx_count, qblock, w_o.shape[1])
    summed = lax.psum_scatter(
        partial_value, ("exp", "head"), scatter_dimension=1, tiled=True
    ).astype(jnp.float32)
    swapped = lax.all_to_all(
        summed.astype(jnp.bfloat16), "ctx", split_axis=0, concat_axis=2, tiled=True
    ).astype(summed.dtype)
    projected = swapped.reshape(tok_dev, D)
    residual_sum = resid.astype(jnp.float32) + projected
    inverse_rms = lax.rsqrt(jnp.mean(residual_sum * residual_sum, axis=1, keepdims=True) + 1e-06)
    normalized = (residual_sum * inverse_rms * norm_gain).astype(jnp.bfloat16)
    experts = lax.axis_size(("exp", "head"))
    top_count = expert_ids.shape[1]
    capacity = max(2, 2 * tok_dev * top_count // experts)
    flat_ids = expert_ids.reshape(-1)
    onehot = (flat_ids[:, None] == jnp.arange(experts, dtype=jnp.int32)[None, :]).astype(jnp.int32)
    slot_rank = jnp.sum((jnp.cumsum(onehot, axis=0) - onehot) * onehot, axis=1)
    target = (flat_ids * capacity + slot_rank).reshape(tok_dev, top_count)
    slot_ids = jnp.arange(experts * capacity, dtype=jnp.int32)
    route_hits = (target[:, :, None] == slot_ids[None, None, :]).astype(jnp.float32)
    picker = jnp.sum(route_hits, axis=1).astype(jnp.bfloat16)
    dispatched = jnp.einsum(
        "ts,td->sd", picker, normalized, preferred_element_type=jnp.float32
    ).astype(jnp.bfloat16)
    outgoing = dispatched.reshape(experts, capacity, D)
    arrived = lax.all_to_all(outgoing, ("exp", "head"), split_axis=0, concat_axis=0, tiled=True)
    rows_in = arrived.reshape(experts * capacity, D)
    gate_local = w_gate[0]
    up_local = w_up[0]
    down_local = w_down[0]
    shard_rows = lax.all_gather(rows_in, "ctx", axis=0, tiled=True)
    gate_part = jnp.dot(shard_rows, gate_local, preferred_element_type=jnp.float32)
    up_part = jnp.dot(shard_rows, up_local, preferred_element_type=jnp.float32)
    hidden_cols = (jax.nn.silu(gate_part) * up_part).astype(jnp.bfloat16)
    expert_cols = jnp.dot(
        lax.all_gather(hidden_cols, "ctx", axis=1, tiled=True),
        down_local,
        preferred_element_type=jnp.float32,
    ).astype(jnp.bfloat16)
    returned = lax.all_to_all(
        expert_cols.reshape(ctx_count, experts * capacity, down_local.shape[1]),
        "ctx",
        split_axis=0,
        concat_axis=2,
        tiled=True,
    )
    returned_rows = lax.all_to_all(
        returned.reshape(experts, capacity, D),
        ("exp", "head"),
        split_axis=0,
        concat_axis=0,
        tiled=True,
    )
    returned_rows = returned_rows.reshape(experts * capacity, D)
    weighted = jnp.sum(route_hits * route_weights[:, :, None], axis=1)
    moe_sum = jnp.dot(weighted, returned_rows.astype(jnp.float32), precision=lax.Precision.HIGHEST)
    return (residual_sum + moe_sum).astype(jnp.bfloat16)


def solution(mesh):
    placed = (
        P(("groups", "ctx"), None),
        P(("groups", "ctx"), ("exp", "head")),
        P(None, ("exp", "head")),
        P(None, ("exp", "head")),
        P(("exp", "head"), "ctx"),
        P(("groups", "ctx", "exp", "head"), None),
        P(),
        P(("exp", "head"), None, "ctx"),
        P(("exp", "head"), None, "ctx"),
        P(("exp", "head"), None, "ctx"),
        P(("groups", "ctx", "exp", "head"), None),
        P(("groups", "ctx", "exp", "head"), None),
    )
    return jax.shard_map(
        shards,
        mesh=mesh,
        in_specs=placed,
        out_specs=P(("groups", "ctx", "exp", "head"), None),
        check_vma=False,
    )
```

profile of v0, /device:TPU:0, one launch (start us, length us, event | category | flops | bytes accessed | tf_op | source)
XLA Modules:
  0.0 148.8 jit_solution(2626256943590443223)
XLA Ops:
  6.6 1.0 reshape.85
  7.7 15.4 %all_gather.12 = bf16[128,576]{1,0:T(8,128)(2,1)S(1)} all-gather(bf16[32,576]{1,0:T(8,128)(2,1)} %param.12), channel_id=1, replica_groups=mesh['groups'=2,'ctx'=4,'exp'=2,'head'=2] {'ctx'}, dimensions={0}, use_global_device_ids=true | all-gather | bytes 184320 | tf_op jit(solution)/shard_map/all_gather | solution.py:36
  23.1 1.3 fusion.19
  24.4 1.3 fusion.18
  25.7 0.2 convolution_bitcast_fusion.1
  25.8 0.3 select_reduce_fusion
  26.1 0.2 convolution_bitcast_fusion
  26.3 0.3 fusion.23
  26.7 13.5 %all_gather.13 = bf16[128,512]{1,0:T(8,128)(2,1)S(1)} all-gather(bf16[32,512]{1,0:T(8,128)(2,1)S(1)} %bitcast.80), channel_id=1, replica_groups=mesh['groups'=2,'ctx'=4,'exp'=2,'head'=2] {'ctx'}, dimensions={0}, use_global_device_ids=true | all-gather | bytes 163840 | tf_op jit(solution)/shard_map/all_gather | solution.py:72
  40.2 0.3 convolution_convert_fusion.1
  40.5 0.1 copy.49
  40.6 0.7 copy.57
  41.6 0.2 select_reduce_fusion.2
  41.9 0.1 copy.47
  42.0 20.8 %reduce-scatter.4.cloned.1.call-done = bf16[8,3584]{1,0:T(8,128)(2,1)} async-done(((bf16[32,3584]{1,0:T(8,128)(2,1)}), bf16[8,3584]{1,0:T(8,128)(2,1)}) %reduce-scatter.4.cloned.1.call-update) | async-done | bytes 57360
  62.8 0.8 reshape.97
  63.6 0.6 copy.50
  64.3 4.6 %all-to-all-start = ((bf16[4,8,896]{2,1,0:T(8,128)(2,1)}), bf16[4,8,896]{2,1,0:T(8,128)(2,1)S(1)}, u32[]{:S(2)}, u32[]{:S(2)}) async-start(bf16[4,8,896]{2,1,0:T(8,128)(2,1)} %copy.50), calls=%async_computation | async-start | bytes 114688 | tf_op jit(solution)/shard_map/all_to_all | solution.py:78
  68.9 5.6 %all-to-all-done = bf16[4,8,896]{2,1,0:T(8,128)(2,1)S(1)} async-done(((bf16[4,8,896]{2,1,0:T(8,128)(2,1)}), bf16[4,8,896]{2,1,0:T(8,128)(2,1)S(1)}, u32[]{:S(2)}, u32[]{:S(2)}) %all-to-all-start) | async-done | bytes 57376 | tf_op jit(solution)/shard_map/all_to_all | solution.py:78
  74.6 0.1 multiply_reduce_fusion
  74.8 0.3 fusion.1
  75.0 8.2 %all_to_all.34 = bf16[4,8,3584]{2,1,0:T(8,128)(2,1)S(1)} all-to-all(bf16[4,8,3584]{2,1,0:T(8,128)(2,1)S(1)} %fusion.1), channel_id=1, replica_groups=mesh['groups'=2,'ctx'=4,'exp'=2,'head'=2] {'exp','head'}, dimensions={0} | all-to-all | bytes 458752 | tf_op jit(solution)/shard_map/all_to_all | solution.py:99
  83.2 19.1 %all_gather.14 = bf16[128,3584]{1,0:T(8,128)(2,1)S(1)} all-gather(bf16[32,3584]{1,0:T(8,128)(2,1)S(1)} %bitcast.77), channel_id=1, replica_groups=mesh['groups'=2,'ctx'=4,'exp'=2,'head'=2] {'ctx'}, dimensions={0}, use_global_device_ids=true | all-gather | bytes 1146880 | tf_op jit(solution)/shard_map/all_gather | solution.py:104
  102.3 2.7 %fusion.7 = f32[128,512]{1,0:T(8,128)S(1)} fusion(bf16[128,3584]{1,0:T(8,128)(2,1)S(1)} %all_gather.14, bf16[1,3584,512]{2,1,0:T(8,128)(2,1)} %param.19), kind=kOutput, calls=%fused_computation.9 | convolution fusion | flops 469762048 | bytes 4849664 | tf_op jit(solution)/shard_map/dot_general | solution.py:105
  105.0 0.6 fusion.15
  105.6 15.8 %all_gather.15 = bf16[128,2048]{1,0:T(8,128)(2,1)S(1)} all-gather(bf16[128,512]{1,0:T(8,128)(2,1)S(1)} %fusion.15), channel_id=1, replica_groups=mesh['groups'=2,'ctx'=4,'exp'=2,'head'=2] {'ctx'}, dimensions={1}, use_global_device_ids=true | all-gather | bytes 655360 | tf_op jit(solution)/shard_map/all_gather | solution.py:109
  121.4 0.7 fusion.9
  122.1 10.7 %all_to_all.35 = bf16[4,32,896]{2,1,0:T(8,128)(2,1)S(1)} all-to-all(bf16[4,32,896]{2,1,0:T(8,128)(2,1)S(1)} %bitcast.78), channel_id=1, replica_groups=mesh['groups'=2,'ctx'=4,'exp'=2,'head'=2] {'ctx'}, dimensions={0} | all-to-all | bytes 458752 | tf_op jit(solution)/shard_map/all_to_all | solution.py:113
  132.9 0.1 copy.48
  133.0 0.1 reshape.91
  133.1 8.0 %all_to_all.36 = bf16[4,8,3584]{2,1,0:T(8,128)(2,1)S(1)} all-to-all(bf16[4,8,3584]{2,1,0:T(8,128)(2,1)S(1)} %reshape.91), channel_id=1, replica_groups=mesh['groups'=2,'ctx'=4,'exp'=2,'head'=2] {'exp','head'}, dimensions={0} | all-to-all | bytes 458752 | tf_op jit(solution)/shard_map/all_to_all | solution.py:120
  141.1 0.8 fusion.2
  (31 shorter events, 0.7 us)
Async XLA Ops:
  6.5 33.7 %copy-start = (bf16[512,896]{1,0:T(8,128)(2,1)S(1)}, bf16[512,896]{1,0:T(8,128)(2,1)}, u32[]{:S(2)}) copy-start(bf16[512,896]{1,0:T(8,128)(2,1)} %param.16) | copy-start | bytes 2752516
  6.5 34.8 %copy-start.4 = (s32[8,2]{0,1:T(2,128)S(1)}, s32[8,2]{0,1:T(2,128)}, u32[]{:S(2)}) copy-start(s32[8,2]{0,1:T(2,128)} %param.22) | copy-start | bytes 196
  6.5 62.3 %copy-start.5 = (f32[8,2]{0,1:T(2,128)S(1)}, f32[8,2]{0,1:T(2,128)}, u32[]{:S(2)}) copy-start(f32[8,2]{0,1:T(2,128)} %param.23) | copy-start | bytes 196
  6.5 68.1 %copy-start.2 = (bf16[8,3584]{1,0:T(8,128)(2,1)S(1)}, bf16[8,3584]{1,0:T(8,128)(2,1)}, u32[]{:S(2)}) copy-start(bf16[8,3584]{1,0:T(8,128)(2,1)} %param.17) | copy-start | bytes 172036
  6.5 68.2 %copy-start.3 = (f32[3584]{0:T(1024)S(1)}, f32[3584]{0:T(1024)}, u32[]{:S(2)}) copy-start(f32[3584]{0:T(1024)} %param.18) | copy-start | bytes 43012
  6.5 56.2 %reduce-scatter.4.cloned.1.call-start = ((), (), s32[]{:S(2)}) async-start(), calls=%async_computation.5 | async-start | bytes 286720
  64.3 10.3 %all-to-all-start = ((bf16[4,8,896]{2,1,0:T(8,128)(2,1)}), bf16[4,8,896]{2,1,0:T(8,128)(2,1)S(1)}, u32[]{:S(2)}, u32[]{:S(2)}) async-start(bf16[4,8,896]{2,1,0:T(8,128)(2,1)} %copy.50), calls=%async_computation | async-start | bytes 114688 | tf_op jit(solution)/shard_map/all_to_all | solution.py:78
  74.6 30.4 %copy-start.6 = (bf16[1,3584,512]{2,1,0:T(8,128)(2,1)S(1)}, bf16[1,3584,512]{2,1,0:T(8,128)(2,1)}, u32[]{:S(2)}) copy-start(bf16[1,3584,512]{2,1,0:T(8,128)(2,1)} %param.20) | copy-start | bytes 11010052
  105.0 16.4 %copy-start.1 = (bf16[1,2048,896]{2,1,0:T(8,128)(2,1)S(1)}, bf16[1,2048,896]{2,1,0:T(8,128)(2,1)}, u32[]{:S(2)}) copy-start(bf16[1,2048,896]{2,1,0:T(8,128)(2,1)} %param.21) | copy-start | bytes 11010052
Sparse Core Ops, SparseCore 0:
  41.5 21.2 reduce-scatter.3
where the time goes:
time: 149 us
  blocking collectives  90.6 us (61%)
  waiting for transfers between devices  26.4 us (18%)
  between operations  13.6 us (9%)
  matrix products  8.65 us (6%)
  starting transfers between devices  4.63 us (3%)
  local copies, waits for them, and re-layouts  3.88 us (3%)
    unnamed x2, waiting for transfers between devices  20.8 us
    all_gather x1, blocking collectives, shards(): shard_rows = lax.all_gather(rows_in, 'ctx', axis=0, tiled=True)  19.1 us
    all_gather x1, blocking collectives, shards(): lax.all_gather(hidden_cols, 'ctx', axis=1, tiled=True)  15.8 us
    all_gather x1, blocking collectives, shards(): shard_rows = lax.all_gather(latent, 'ctx', axis=0, tiled=True)  15.4 us
    all_gather x1, blocking collectives, shards(): lax.all_gather(attended, 'ctx', axis=0, tiled=True)  13.5 us
    all_to_all x1, blocking collectives, shards(): lax.all_to_all(expert_cols.reshape(ctx_count, experts * capacity, down_lo...  10.7 us
    all_to_all x1, blocking collectives, shards(): lax.all_to_all(outgoing, ('exp', 'head'), split_axis=0, concat_axis=0, ti...  8.16 us
    all_to_all x1, blocking collectives, shards(): lax.all_to_all(returned.reshape(experts, capacity, D), ('exp', 'head'), s...  8.03 us
  transfers between devices with their start and end apart: 2, of which 2 were waited for; matrix products, arithmetic and copies ran while one was open for 0% of the time, Pallas kernels for 0%

commit v1 on v0

--- a/solution.py
+++ b/solution.py
@@ -8,6 +8,28 @@
 NOPE = 128
 ROPE = 64
 LATENT = 512
+
+
+def split_up(x, dim, count):
+    before, after = (x.shape[:dim], x.shape[dim + 1 :])
+    return jnp.moveaxis(x.reshape(*before, count, -1, *after), dim, 0)
+
+
+def laid_out(parts, dim):
+    shape = list(parts.shape[1:])
+    shape[dim] *= parts.shape[0]
+    return jnp.moveaxis(parts, 0, dim).reshape(shape)
+
+
+def swapped_with_each(x, axis, split_dim, concat_dim):
+    count, mine = (lax.axis_size(axis), lax.axis_index(axis))
+    parts = split_up(x, split_dim, count)
+    done = [parts[mine]]
+    for lap in range(1, count):
+        sent = parts[mine ^ lap]
+        done.append(lax.ppermute(sent, axis, [(i, i ^ lap) for i in range(count)]))
+    parts = jnp.stack(done)[mine ^ jnp.arange(count)]
+    return laid_out(parts, concat_dim)
 
 
 def shards(
@@ -75,9 +97,7 @@
     summed = lax.psum_scatter(
         partial_value, ("exp", "head"), scatter_dimension=1, tiled=True
     ).astype(jnp.float32)
-    swapped = lax.all_to_all(
-        summed.astype(jnp.bfloat16), "ctx", split_axis=0, concat_axis=2, tiled=True
-    ).astype(summed.dtype)
+    swapped = swapped_with_each(summed.astype(jnp.bfloat16), "ctx", 0, 2).astype(summed.dtype)
     projected = swapped.reshape(tok_dev, D)
     residual_sum = resid.astype(jnp.float32) + projected
     inverse_rms = lax.rsqrt(jnp.mean(residual_sum * residual_sum, axis=1, keepdims=True) + 1e-06)

time: 149 us -> 147 us (0.987)
  waiting for transfers between devices: 26.4 us -> 24.2 us
    all_to_all x1 -> x0, waiting for transfers between devices: 5.64 us -> none  [shards(): lax.all_to_all(summed.astype(jnp.bfloat16), 'ctx', split_axis=0, concat_a...]
    all_to_all x1 -> x0, starting transfers between devices: 4.59 us -> none  [shards(): lax.all_to_all(summed.astype(jnp.bfloat16), 'ctx', split_axis=0, concat_a...]
    ppermute x0 -> x3, starting transfers between devices: none -> 4.45 us  [swapped_with_each(): done.append(lax.ppermute(sent, axis, [(i, i ^ lap) for i in range(count)]))]
    ppermute x0 -> x3, waiting for transfers between devices: none -> 3.54 us  [swapped_with_each(): done.append(lax.ppermute(sent, axis, [(i, i ^ lap) for i in range(count)]))]
  transfers between devices with their start and end apart: 2 -> 4, of which waited for: 2 -> 4; matrix products, arithmetic and copies ran while one was open for 0% -> 0% of each run, Pallas kernels for 0% -> 0%
where the time goes in v1:
time: 147 us
  blocking collectives  90.8 us (62%)
  waiting for transfers between devices  24.2 us (16%)
  between operations  13.7 us (9%)
  matrix products  8.65 us (6%)
  starting transfers between devices  4.49 us (3%)
  local copies, waits for them, and re-layouts  3.96 us (3%)
    unnamed x2, waiting for transfers between devices  20.7 us
    all_gather x1, blocking collectives, shards(): shard_rows = lax.all_gather(rows_in, 'ctx', axis=0, tiled=True)  19.7 us
    all_gather x1, blocking collectives, shards(): lax.all_gather(hidden_cols, 'ctx', axis=1, tiled=True)  16 us
    all_gather x1, blocking collectives, shards(): shard_rows = lax.all_gather(latent, 'ctx', axis=0, tiled=True)  15.4 us
    all_gather x1, blocking collectives, shards(): lax.all_gather(attended, 'ctx', axis=0, tiled=True)  13.5 us
    all_to_all x1, blocking collectives, shards(): lax.all_to_all(expert_cols.reshape(ctx_count, experts * capacity, down_lo...  9.98 us
    all_to_all x1, blocking collectives, shards(): lax.all_to_all(outgoing, ('exp', 'head'), split_axis=0, concat_axis=0, ti...  8.16 us
    all_to_all x1, blocking collectives, shards(): lax.all_to_all(returned.reshape(experts, capacity, D), ('exp', 'head'), s...  8.03 us
  transfers between devices with their start and end apart: 4, of which 4 were waited for; matrix products, arithmetic and copies ran while one was open for 0% of the time, Pallas kernels for 0%

profile of v1, /device:TPU:0, one launch (start us, length us, event | category | flops | bytes accessed | tf_op | source)
XLA Modules:
  0.0 146.8 jit_solution(5247143959769553894)
XLA Ops:
  6.6 1.0 reshape.108
  7.7 15.4 %all_gather.12 = bf16[128,576]{1,0:T(8,128)(2,1)S(1)} all-gather(bf16[32,576]{1,0:T(8,128)(2,1)} %param.12), channel_id=1, replica_groups=mesh['groups'=2,'ctx'=4,'exp'=2,'head'=2] {'ctx'}, dimensions={0}, use_global_device_ids=true | all-gather | bytes 184320 | tf_op jit(solution)/shard_map/all_gather | solution.py:58
  23.1 1.3 fusion.19
  24.4 1.3 fusion.18
  25.7 0.2 convolution_bitcast_fusion.1
  25.8 0.3 select_reduce_fusion
  26.1 0.2 convolution_bitcast_fusion
  26.3 0.3 fusion.23
  26.7 13.5 %all_gather.13 = bf16[128,512]{1,0:T(8,128)(2,1)S(1)} all-gather(bf16[32,512]{1,0:T(8,128)(2,1)S(1)} %bitcast.90), channel_id=1, replica_groups=mesh['groups'=2,'ctx'=4,'exp'=2,'head'=2] {'ctx'}, dimensions={0}, use_global_device_ids=true | all-gather | bytes 163840 | tf_op jit(solution)/shard_map/all_gather | solution.py:94
  40.2 0.3 convolution_convert_fusion.1
  40.6 0.7 copy.61
  41.6 0.2 select_reduce_fusion.2
  42.1 20.7 %reduce-scatter.4.cloned.1.call-done = bf16[8,3584]{1,0:T(8,128)(2,1)} async-done(((bf16[32,3584]{1,0:T(8,128)(2,1)}), bf16[8,3584]{1,0:T(8,128)(2,1)}) %reduce-scatter.4.cloned.1.call-update) | async-done | bytes 57360
  62.8 0.8 reshape.130
  63.6 0.1 constant_dynamic-slice_fusion.3
  63.8 3.4 %collective-permute-start.2 = (bf16[1,8,896]{2,1,0:T(8,128)(2,1)S(1)}, bf16[1,8,896]{2,1,0:T(8,128)(2,1)S(1)}, u32[]{:S(2)}, u32[]{:S(2)}) collective-permute-start(bf16[1,8,896]{2,1,0:T(8,128)(2,1)S(1)} %copy.57), channel_id=1, source_target_pairs={{0,12},{4,8},{8,4},{12,0},{1,13},{5,9},{9,5},{13,1},{2,14},{6,10},... | collective-permute-start | bytes 43016 | tf_op jit(solution)/shard_map/ppermute | solution.py:30
  67.2 1.1 collective-permute-start.1
  68.3 1.1 collective-permute-done.2
  69.4 1.5 %collective-permute-done = bf16[1,8,896]{2,1,0:T(8,128)(2,1)S(1)} collective-permute-done((bf16[1,8,896]{2,1,0:T(8,128)(2,1)S(1)}, bf16[1,8,896]{2,1,0:T(8,128)(2,1)S(1)}, u32[]{:S(2)}, u32[]{:S(2)}) %collective-permute-start) | collective-permute-done | bytes 14368 | tf_op jit(solution)/shard_map/ppermute | solution.py:30
  70.9 0.9 collective-permute-done.1
  71.8 0.6 gather_fusion
  72.4 0.1 multiply_reduce_fusion
  72.6 0.3 fusion.1
  72.9 8.2 %all_to_all.25 = bf16[4,8,3584]{2,1,0:T(8,128)(2,1)S(1)} all-to-all(bf16[4,8,3584]{2,1,0:T(8,128)(2,1)S(1)} %fusion.1), channel_id=1, replica_groups=mesh['groups'=2,'ctx'=4,'exp'=2,'head'=2] {'exp','head'}, dimensions={0} | all-to-all | bytes 458752 | tf_op jit(solution)/shard_map/all_to_all | solution.py:119
  81.0 19.7 %all_gather.14 = bf16[128,3584]{1,0:T(8,128)(2,1)S(1)} all-gather(bf16[32,3584]{1,0:T(8,128)(2,1)S(1)} %bitcast.87), channel_id=1, replica_groups=mesh['groups'=2,'ctx'=4,'exp'=2,'head'=2] {'ctx'}, dimensions={0}, use_global_device_ids=true | all-gather | bytes 1146880 | tf_op jit(solution)/shard_map/all_gather | solution.py:124
  100.7 2.7 %fusion.7 = f32[128,512]{1,0:T(8,128)S(1)} fusion(bf16[128,3584]{1,0:T(8,128)(2,1)S(1)} %all_gather.14, bf16[1,3584,512]{2,1,0:T(8,128)(2,1)} %param.19), kind=kOutput, calls=%fused_computation.10 | convolution fusion | flops 469762048 | bytes 4849664 | tf_op jit(solution)/shard_map/dot_general | solution.py:125
  103.4 0.6 fusion.15
  104.1 16.0 %all_gather.15 = bf16[128,2048]{1,0:T(8,128)(2,1)S(1)} all-gather(bf16[128,512]{1,0:T(8,128)(2,1)S(1)} %fusion.15), channel_id=1, replica_groups=mesh['groups'=2,'ctx'=4,'exp'=2,'head'=2] {'ctx'}, dimensions={1}, use_global_device_ids=true | all-gather | bytes 655360 | tf_op jit(solution)/shard_map/all_gather | solution.py:129
  120.1 0.7 fusion.9
  120.8 10.0 %all_to_all.26 = bf16[4,32,896]{2,1,0:T(8,128)(2,1)S(1)} all-to-all(bf16[4,32,896]{2,1,0:T(8,128)(2,1)S(1)} %bitcast.88), channel_id=1, replica_groups=mesh['groups'=2,'ctx'=4,'exp'=2,'head'=2] {'ctx'}, dimensions={0} | all-to-all | bytes 458752 | tf_op jit(solution)/shard_map/all_to_all | solution.py:133
  131.0 8.0 %all_to_all.27 = bf16[4,8,3584]{2,1,0:T(8,128)(2,1)S(1)} all-to-all(bf16[4,8,3584]{2,1,0:T(8,128)(2,1)S(1)} %reshape.114), channel_id=1, replica_groups=mesh['groups'=2,'ctx'=4,'exp'=2,'head'=2] {'exp','head'}, dimensions={0} | all-to-all | bytes 458752 | tf_op jit(solution)/shard_map/all_to_all | solution.py:140
  139.1 0.8 fusion.2
  (43 shorter events, 1.1 us)
Async XLA Ops:
  6.5 33.7 %copy-start = (bf16[512,896]{1,0:T(8,128)(2,1)S(1)}, bf16[512,896]{1,0:T(8,128)(2,1)}, u32[]{:S(2)}) copy-start(bf16[512,896]{1,0:T(8,128)(2,1)} %param.16) | copy-start | bytes 2752516
  6.5 34.8 %copy-start.4 = (s32[8,2]{0,1:T(2,128)S(1)}, s32[8,2]{0,1:T(2,128)}, u32[]{:S(2)}) copy-start(s32[8,2]{0,1:T(2,128)} %param.22) | copy-start | bytes 196
  6.5 35.5 %copy-start.5 = (f32[8,2]{0,1:T(2,128)S(1)}, f32[8,2]{0,1:T(2,128)}, u32[]{:S(2)}) copy-start(f32[8,2]{0,1:T(2,128)} %param.23) | copy-start | bytes 196
  6.5 65.9 %copy-start.2 = (bf16[8,3584]{1,0:T(8,128)(2,1)S(1)}, bf16[8,3584]{1,0:T(8,128)(2,1)}, u32[]{:S(2)}) copy-start(bf16[8,3584]{1,0:T(8,128)(2,1)} %param.17) | copy-start | bytes 172036
  6.5 66.0 %copy-start.3 = (f32[3584]{0:T(1024)S(1)}, f32[3584]{0:T(1024)}, u32[]{:S(2)}) copy-start(f32[3584]{0:T(1024)} %param.18) | copy-start | bytes 43012
  6.5 56.2 %reduce-scatter.4.cloned.1.call-start = ((), (), s32[]{:S(2)}) async-start(), calls=%async_computation.4 | async-start | bytes 286720
  63.8 5.6 %collective-permute-start.2 = (bf16[1,8,896]{2,1,0:T(8,128)(2,1)S(1)}, bf16[1,8,896]{2,1,0:T(8,128)(2,1)S(1)}, u32[]{:S(2)}, u32[]{:S(2)}) collective-permute-start(bf16[1,8,896]{2,1,0:T(8,128)(2,1)S(1)} %copy.57), channel_id=1, source_target_pairs={{0,12},{4,8},{8,4},{12,0},{1,13},{5,9},{9,5},{13,1},{2,14},{6,10},... | collective-permute-start | bytes 43016 | tf_op jit(solution)/shard_map/ppermute | solution.py:30
  67.2 3.7 %collective-permute-start = (bf16[1,8,896]{2,1,0:T(8,128)(2,1)S(1)}, bf16[1,8,896]{2,1,0:T(8,128)(2,1)S(1)}, u32[]{:S(2)}, u32[]{:S(2)}) collective-permute-start(bf16[1,8,896]{2,1,0:T(8,128)(2,1)S(1)} %copy.55), channel_id=1, source_target_pairs={{0,4},{4,0},{8,12},{12,8},{1,5},{5,1},{9,13},{13,9},{2,6},{6,2},{1... | collective-permute-start | bytes 43016 | tf_op jit(solution)/shard_map/ppermute | solution.py:30
  67.2 4.6 %collective-permute-start.1 = (bf16[1,8,896]{2,1,0:T(8,128)(2,1)S(1)}, bf16[1,8,896]{2,1,0:T(8,128)(2,1)S(1)}, u32[]{:S(2)}, u32[]{:S(2)}) collective-permute-start(bf16[1,8,896]{2,1,0:T(8,128)(2,1)S(1)} %copy.56), channel_id=1, source_target_pairs={{0,8},{4,12},{8,0},{12,4},{1,9},{5,13},{9,1},{13,5},{2,10},{6,14},... | collective-permute-start | bytes 43016 | tf_op jit(solution)/shard_map/ppermute | solution.py:30
  72.4 31.0 %copy-start.6 = (bf16[1,3584,512]{2,1,0:T(8,128)(2,1)S(1)}, bf16[1,3584,512]{2,1,0:T(8,128)(2,1)}, u32[]{:S(2)}) copy-start(bf16[1,3584,512]{2,1,0:T(8,128)(2,1)} %param.20) | copy-start | bytes 11010052
  103.4 16.7 %copy-start.1 = (bf16[1,2048,896]{2,1,0:T(8,128)(2,1)S(1)}, bf16[1,2048,896]{2,1,0:T(8,128)(2,1)}, u32[]{:S(2)}) copy-start(bf16[1,2048,896]{2,1,0:T(8,128)(2,1)} %param.21) | copy-start | bytes 11010052
Sparse Core Ops, SparseCore 0:
  41.5 21.2 reduce-scatter.3
